TPU v7x, 32 devices: a whole 2x2x4 slice. The times are simulated.
32 devices in a mesh: grp: 2 (over x), seq: 16 (over z, y, core).
Axes of the slice: x: 2, y: 2, z: 4, core: 2. Of those that a mesh axis runs over, the one named last changes fastest.
Arguments:
- conv_input: bfloat16 [8192, 4352], P(('grp', 'seq')), parts along dimension 0, may hold values from -6 to 6, as said below
- conv_weight: float32 [4, 4352], replicated, may hold values from -3 to 3
- step_logit: float32 [8192, 32], P(('grp', 'seq')), parts along dimension 0, may hold values from -20 to 0, as said below
- decay_log: float32 [32], replicated, may hold values from -0.5 to 0.5
- skip_gain: float32 [32], replicated, may hold values from 0.5 to 2
Outputs:
- mixer_out: bfloat16 [8192, 4096], P(('grp', 'seq')), parts along dimension 0
There are 2 independent parts, one for each index of `grp`. A program takes and returns all parts, laid end to end along the dimension named above; an argument that names none is the same for every part. Nothing has to cross between parts.
Inputs may be any that keep to these rules, and one draw needn't show every extreme that they name: `conv_input`: activations before the convolution. `step_logit`: step sizes before softplus.
All inputs are finite; a program needn't handle non-finite values.
Results may differ from a plain program's by a relative error of at most 0.0047.
Values may be sent and summed in bfloat16 or wider, within the bound.
A program may use at most 128 MiB of HBM per device.

v0:
```python
import jax
import jax.numpy as jnp
from jax import lax
from jax.sharding import PartitionSpec as P

HEADDIM = 128
STATE = 128
GROUP = 256


def as_sent(shard):

    def short(part):
        return part.astype(jnp.bfloat16) if part.dtype == jnp.float32 else part

    return jax.tree.map(short, shard)


def from_behind(value, axis, steps):
    count = lax.axis_size(axis)
    leading, last = (max(0, -steps), min(count, count - steps))
    return lax.ppermute(value, axis, [(source, source + steps) for source in range(leading, last)])


def conv_activate(extended, kernel, row_count):
    running = kernel[0] * extended[0:row_count].astype(jnp.float32)
    for tap_index in range(1, kernel.shape[0]):
        running = running + kernel[tap_index] * extended[tap_index : tap_index + row_count].astype(
            jnp.float32
        )
    return jax.nn.silu(running).astype(jnp.bfloat16)


def group_terms(activated, logits, decay_rate, skip_gain):
    head_count = decay_rate.shape[0]
    inner_width = head_count * HEADDIM
    block_count = activated.shape[0]
    span_rows = activated.shape[1]
    values = activated[:, :, :inner_width].reshape(block_count, span_rows, head_count, HEADDIM)
    b_rows = activated[:, :, inner_width : inner_width + STATE]
    c_rows = activated[:, :, inner_width + STATE :]
    time_step_size = jax.nn.softplus(logits)
    cum_decay = jnp.cumsum(time_step_size * decay_rate, axis=1)
    decay_t = jnp.transpose(cum_decay, (0, 2, 1))
    step_t = jnp.transpose(time_step_size, (0, 2, 1))
    scores = jnp.einsum("cqn,csn->cqs", c_rows, b_rows, preferred_element_type=jnp.float32)
    token_position = jnp.arange(span_rows)
    causal = token_position[:, None] >= token_position[None, :]
    decay_gap = jnp.where(causal, decay_t[:, :, :, None] - decay_t[:, :, None, :], -jnp.inf)
    weights = (scores[:, None] * jnp.exp(decay_gap) * step_t[:, :, None, :]).astype(jnp.bfloat16)
    intra_out = jnp.einsum("chqs,cshp->cqhp", weights, values, preferred_element_type=jnp.float32)
    local_out = intra_out + skip_gain[:, None] * values.astype(jnp.float32)
    tail_weight = jnp.transpose(jnp.exp(decay_t[:, :, -1:] - decay_t) * step_t, (0, 2, 1))
    weighted = (values * tail_weight[..., None]).astype(jnp.bfloat16)
    states = jnp.einsum("cshp,csn->chpn", weighted, b_rows, preferred_element_type=jnp.float32)
    return (local_out, states, cum_decay, c_rows)


def split_parts(state_field):
    upper_part = lax.optimization_barrier(state_field.astype(jnp.bfloat16))
    lower_part = (state_field - upper_part.astype(jnp.float32)).astype(jnp.bfloat16)
    return (upper_part, lower_part)


def state_readout(form, c_rows, state_field):
    upper_part, lower_part = split_parts(state_field)
    upper_term = jnp.einsum(form, c_rows, upper_part, preferred_element_type=jnp.float32)
    lower_term = jnp.einsum(form, c_rows, lower_part, preferred_element_type=jnp.float32)
    return upper_term + lower_term


def chain_states(initial, group_ends, states):

    def advance(current, pieces):
        end_log, piece = pieces
        return (jnp.exp(end_log)[:, None, None] * current + piece, current)

    final_state, entering = lax.scan(advance, initial, (group_ends, states))
    return (entering, final_state)


def carry_state(device_log, final_state):
    head_count = device_log.shape[0]
    all_logs = lax.all_gather(device_log[None, :], "seq", axis=0, tiled=True)
    flat_state = final_state.reshape(1, head_count * HEADDIM, STATE)
    received = lax.all_to_all(
        flat_state.astype(jnp.bfloat16), "seq", split_axis=1, concat_axis=0, tiled=True
    ).astype(flat_state.dtype)
    source_count = received.shape[0]
    row_count = received.shape[1]
    first_row = lax.axis_index("seq") * row_count
    head_of = (first_row + jnp.arange(row_count, dtype=jnp.int32)) // HEADDIM
    head_pick = (head_of[:, None] == jnp.arange(head_count, dtype=jnp.int32)[None, :]).astype(
        jnp.float32
    )
    row_logs = jnp.dot(all_logs, head_pick.T, precision=lax.Precision.HIGHEST)
    total_log = jnp.cumsum(row_logs, axis=0)
    before_log = total_log - row_logs
    source_order = jnp.arange(source_count)
    earlier_mask = source_order[None, :] < source_order[:, None]
    exponent = jnp.where(
        earlier_mask[:, :, None], before_log[:, None, :] - total_log[None, :, :], -jnp.inf
    )
    mixed = jnp.einsum("sjr,jrn->srn", jnp.exp(exponent), received, precision=lax.Precision.HIGHEST)
    returned = lax.all_to_all(
        as_sent(mixed), "seq", split_axis=0, concat_axis=1, tiled=True
    ).astype(mixed.dtype)
    return returned.reshape(head_count, HEADDIM, STATE)


def on_device(conv_input, conv_weight, step_logit, decay_log, skip_gain):
    tap_count = conv_weight.shape[0]
    row_count = conv_input.shape[0]
    edge_rows = conv_input[row_count - (tap_count - 1) :]
    previous = from_behind(edge_rows, "seq", 1)
    extended = jnp.concatenate([previous, conv_input], 0)
    block_count = row_count // GROUP
    activated = conv_activate(extended, conv_weight, row_count).reshape(block_count, GROUP, -1)
    logits = step_logit.reshape(block_count, GROUP, -1)
    decay_rate = -jnp.exp(decay_log)
    local_out, states, cum_decay, c_rows = group_terms(activated, logits, decay_rate, skip_gain)
    group_ends = cum_decay[:, -1, :]
    device_log = jnp.sum(group_ends, axis=0)
    empty_state = jnp.zeros_like(states[0])
    _, final_state = chain_states(empty_state, group_ends, states)
    incoming = carry_state(device_log, final_state)
    entering, _ = chain_states(incoming, group_ends, states)
    inter_out = jnp.exp(cum_decay)[..., None] * state_readout("cqn,chpn->cqhp", c_rows, entering)
    result = local_out + inter_out
    return result.reshape(row_count, -1).astype(jnp.bfloat16)


def solution(mesh):
    return jax.shard_map(
        on_device,
        mesh=mesh,
        in_specs=(P(("grp", "seq"), None), P(), P(("grp", "seq"), None), P(), P()),
        out_specs=P(("grp", "seq"), None),
        check_vma=False,
    )
```

profile of v0, /device:TPU:9, one launch (start us, length us, event | category | flops | bytes accessed | tf_op | source)
XLA Modules:
  0.0 161.1 jit_solution(3897748167165078665)
XLA Ops:
  0.0 0.9 slice.46
  0.9 3.7 %collective-permute-start = (bf16[3,4352]{1,0:T(4,128)(2,1)S(1)}, bf16[3,4352]{1,0:T(4,128)(2,1)S(1)}, u32[]{:S(2)}, u32[]{:S(2)}) collective-permute-start(bf16[3,4352]{1,0:T(4,128)(2,1)S(1)} %slice.46), channel_id=1, source_target_pairs={{0,1},{1,2},{2,3},{3,4},{4,5},{5,6},{6,7},{7,8},{8,9},{9,10},{10,1... | collective-permute-start | bytes 78344 | tf_op jit(solution)/shard_map/ppermute | solution.py:22
  4.6 0.7 exponential_negate_fusion
  5.3 0.8 compare_select_fusion
  6.1 0.6 reduce-window.6
  6.7 0.2 slice_reduce_fusion
  6.9 0.1 copy.44
  7.0 0.1 broadcast.128
  7.1 0.1 bitcast_exponential_fusion
  7.2 0.5 slice_reduce_fusion.5
  7.7 0.5 fusion.49
  8.2 0.1 broadcast_bitcast_fusion
  8.3 0.1 multiply_bitcast_fusion
  8.4 1.2 slice_reduce_fusion.4
  9.6 0.1 copy.55
  9.7 2.5 %mul.190 = f32[256,32,128]{2,1,0:T(8,128)} broadcast(f32[256,32]{1,0:T(8,128)S(1)} %bitcast.104), dimensions={0,1} | broadcast | bytes 4227072 | tf_op jit(solution)/shard_map/mul | solution.py:54
  12.3 5.0 %mul.191 = f32[1,256,4096]{2,1,0:T(8,128)} reshape(f32[256,32,128]{2,1,0:T(8,128)} %mul.190) | data formatting | bytes 8388608 | tf_op jit(solution)/shard_map/mul | solution.py:54
  17.3 0.0 collective-permute-done
  17.3 6.1 %fusion.13 = bf16[1,256,4352]{2,1,0:T(8,128)(2,1)S(1)} fusion(bf16[256,4352]{1,0:T(8,128)(2,1)} %param.5, f32[4352]{0:T(1024)S(1)} %get-tuple-element.27, bf16[3,4352]{1,0:T(4,128)(2,1)S(1)} %collective-permute-done, f32[4352]{0:T(1024)S(1)} %get-tuple-element.28, f32[4352]{0:T(1024)S(1)} %get-tuple-element.26, f32[4352]{0:T(1024)S(1)} %get-tuple-element.20), kind=kLoop, calls=%fused_computation.21 | loop fusion | flops 27852800 | bytes 4552192 | tf_op jit(solution)/shard_map/reshape | solution.py:118
  23.4 0.0 copy-done
  23.4 0.6 fusion.14
  24.0 0.5 copy.62
  24.5 3.0 %fusion.1 = bf16[1,4096,128]{2,1,0:T(8,128)(2,1)S(1)} fusion(bf16[32,8,32,128]{3,2,1,0:T(8,128)(2,1)S(1)} %copy.62, f32[4096]{0:T(1024)S(1)} %broadcast_bitcast_fusion, bf16[1,256,4352]{2,1,0:T(8,128)(2,1)S(1)} %fusion.13), kind=kOutput, calls=%fused_computation.3 | convolution fusion | flops 269484032 | bytes 3227648 | tf_op jit(solution)/shard_map/cshp,csn->chpn/dot_general | solution.py:55
  27.5 17.0 %copy.79 = bf16[1,4096,128]{2,0,1:T(2,128)(2,1)} copy(bf16[1,4096,128]{2,1,0:T(8,128)(2,1)S(1)} %fusion.1) | data formatting | bytes 2097152 | tf_op jit(solution)/shard_map/convert_element_type | solution.py:87
  44.5 0.6 broadcast.138
  45.1 23.7 %reduce.14 = bf16[4096,128]{1,0:T(8,128)(2,1)S(1)} reduce(bf16[4096,1,128]{2,1,0:T(2,128)(2,1)} %bitcast.99, bf16[]{:T(256)} %broadcast.138), dimensions={1}, to_apply=%bitcast.95.reduce_sub_computation | reduce | bytes 2097154
  68.8 1.1 reshape.321
  69.9 5.1 %all-to-all-start = ((bf16[16,2,16384]{2,1,0:T(2,128)(2,1)}), bf16[16,2,16384]{2,1,0:T(2,128)(2,1)S(1)}, u32[]{:S(2)}, u32[]{:S(2)}) async-start(bf16[16,2,16384]{2,1,0:T(2,128)(2,1)} %reshape.321), calls=%async_computation | async-start | bytes 2097152 | tf_op jit(solution)/shard_map/all_to_all | solution.py:86
  75.0 0.1 copy.49
  75.1 35.0 %all-gather = f32[16,1,32]{2,1,0:T(1,128)S(1)} all-gather(f32[1,1,32]{2,1,0:T(1,128)S(1)} %copy.49), channel_id=2, replica_groups=mesh['grp'=2,'seq'=16] {'seq'}, dimensions={0}, use_global_device_ids=true | all-gather | bytes 2176 | tf_op jit(solution)/shard_map/all_gather | solution.py:84
  110.1 0.2 fusion.37
  110.3 0.1 reduce_window_sum.48
  110.4 0.6 sub.66
  111.0 0.1 copy.51
  111.1 1.5 copy.50
  112.5 0.0 all-to-all-done
  112.5 3.4 %reshape.322 = bf16[4096,1,128]{2,1,0:T(2,128)(2,1)} reshape(bf16[16,2,16384]{2,1,0:T(2,128)(2,1)S(1)} %all-to-all-done) | data formatting | bytes 2097152
  116.0 1.7 %copy.58 = bf16[1,4096,128]{2,1,0:T(8,128)(2,1)S(1)} copy(bf16[1,4096,128]{2,0,1:T(2,128)(2,1)} %bitcast.98) | data formatting | bytes 2097152
  117.7 3.9 %fusion.24 = bf16[16,256,128]{2,0,1:T(8,128)(2,1)S(1)} fusion(bf16[16,256,128]{2,1,0:T(8,128)(2,1)S(1)} %bitcast.103, f32[16,256]{0,1:T(8,128)S(1)} %copy.51, f32[16,256]{0,1:T(8,128)} %copy.50, pred[16,16]{1,0:T(8,128)(4,1)S(1)} %iota_compare_fusion.3), kind=kOutput, calls=%fused_computation.31 | convolution fusion | flops 101318656 | bytes 2130176 | tf_op jit(solution)/shard_map/sjr,jrn->srn/dot_general | solution.py:104
  121.7 1.2 copy.53
  122.9 4.1 %all-to-all-start.1 = ((bf16[16,256,128]{2,1,0:T(8,128)(2,1)}), bf16[16,256,128]{2,1,0:T(8,128)(2,1)S(1)}, u32[]{:S(2)}, u32[]{:S(2)}) async-start(bf16[16,256,128]{2,1,0:T(8,128)(2,1)} %copy.53), calls=%async_computation.1 | async-start | bytes 2097152 | tf_op jit(solution)/shard_map/all_to_all | solution.py:105
  127.1 0.6 copy.77
  127.7 0.6 copy.78
  128.3 0.6 iota_compare_fusion
  129.0 0.6 bitcast_add_fusion.1
  129.6 3.2 %fusion.48 = (bf16[1,256,4096]{2,1,0:T(8,128)(2,1)}, f32[1,256,4096]{2,1,0:T(8,128)}) fusion(bf16[1,256,4352]{2,1,0:T(8,128)(2,1)S(1)} %fusion.13), kind=kLoop, calls=%fused_computation.80 | loop fusion | flops 1048576 | bytes 8388608 | tf_op jit(solution)/shard_map/slice | solution.py:39
  132.8 4.1 %copy.41 = bf16[1,256,4096]{1,2,0:T(8,128)(2,1)} copy(bf16[1,256,4096]{2,1,0:T(8,128)(2,1)} %get-tuple-element.36) | data formatting | bytes 4194304 | tf_op jit(solution)/shard_map/slice | solution.py:39
  136.8 5.6 %copy.45 = f32[1,256,4096]{1,2,0:T(8,128)} copy(f32[1,256,4096]{2,1,0:T(8,128)} %get-tuple-element.38) | data formatting | bytes 8388608 | tf_op jit(solution)/shard_map/convert_element_type | solution.py:52
  142.5 0.2 fusion.40
  142.6 9.3 %all-to-all-done.1 = bf16[16,256,128]{2,1,0:T(8,128)(2,1)S(1)} async-done(((bf16[16,256,128]{2,1,0:T(8,128)(2,1)}), bf16[16,256,128]{2,1,0:T(8,128)(2,1)S(1)}, u32[]{:S(2)}, u32[]{:S(2)}) %all-to-all-start.1) | async-done | bytes 1048608 | tf_op jit(solution)/shard_map/all_to_all | solution.py:105
  151.9 0.0 copy-start.5
  151.9 0.0 copy-start.6
  151.9 0.0 copy-start.7
  152.0 0.7 fusion.28
  152.7 0.7 fusion.30
  153.4 0.7 copy-done.1
  154.1 0.7 copy-done.2
  154.8 0.0 copy-done.3
  154.8 0.0 copy-done.4
  154.8 0.0 copy-done.5
  154.8 0.0 copy-done.6
  154.8 0.0 copy-done.7
  154.8 3.4 %fusion.4 = bf16[1,256,32,128]{1,3,2,0:T(8,128)(2,1)S(1)} fusion(f32[256,32,128]{0,2,1:T(8,128)S(1)} %fusion.30, f32[256,32,128]{0,2,1:T(8,128)S(1)} %fusion.28, f32[1,256,32,128]{1,3,2,0:T(8,128)S(1)} %bitcast.100, f32[256,32]{0,1:T(8,128)S(1)} %bitcast.111, f32[32]{0:T(128)S(1)} %copy-done.7, bf16[256,32,128]{0,2,1:T(8,128)(2,1)S(1)} %bitcast.101, ...), kind=kOutput, calls=%fused_computation.8 | convolution fusion | flops 553648128 | bytes 17203328 | tf_op jit(solution)/shard_map/chqs,cshp->cqhp/dot_general | solution.py:51
  158.2 2.9 %copy.54 = bf16[256,4096]{1,0:T(8,128)(2,1)} copy(bf16[256,4096]{0,1:T(8,128)(2,1)S(1)} %bitcast.102) | data formatting | bytes 4194304 | tf_op jit(solution)/shard_map/convert_element_type | solution.py:130
  (13 shorter events, 0.2 us)
Async XLA Ops:
  0.9 16.4 %collective-permute-start = (bf16[3,4352]{1,0:T(4,128)(2,1)S(1)}, bf16[3,4352]{1,0:T(4,128)(2,1)S(1)}, u32[]{:S(2)}, u32[]{:S(2)}) collective-permute-start(bf16[3,4352]{1,0:T(4,128)(2,1)S(1)} %slice.46), channel_id=1, source_target_pairs={{0,1},{1,2},{2,3},{3,4},{4,5},{5,6},{6,7},{7,8},{8,9},{9,10},{10,1... | collective-permute-start | bytes 78344 | tf_op jit(solution)/shard_map/ppermute | solution.py:22
  17.3 6.1 %copy-start = (f32[1,256,4096]{2,1,0:T(8,128)S(1)}, f32[1,256,4096]{2,1,0:T(8,128)}, u32[]{:S(2)}) copy-start(f32[1,256,4096]{2,1,0:T(8,128)} %mul.191) | copy-start | bytes 12582916
  69.9 42.7 %all-to-all-start = ((bf16[16,2,16384]{2,1,0:T(2,128)(2,1)}), bf16[16,2,16384]{2,1,0:T(2,128)(2,1)S(1)}, u32[]{:S(2)}, u32[]{:S(2)}) async-start(bf16[16,2,16384]{2,1,0:T(2,128)(2,1)} %reshape.321), calls=%async_computation | async-start | bytes 2097152 | tf_op jit(solution)/shard_map/all_to_all | solution.py:86
  122.9 29.0 %all-to-all-start.1 = ((bf16[16,256,128]{2,1,0:T(8,128)(2,1)}), bf16[16,256,128]{2,1,0:T(8,128)(2,1)S(1)}, u32[]{:S(2)}, u32[]{:S(2)}) async-start(bf16[16,256,128]{2,1,0:T(8,128)(2,1)} %copy.53), calls=%async_computation.1 | async-start | bytes 2097152 | tf_op jit(solution)/shard_map/all_to_all | solution.py:105
  151.9 2.2 %copy-start.1 = (f32[1,256,4096]{1,2,0:T(8,128)S(1)}, f32[1,256,4096]{1,2,0:T(8,128)}, u32[]{:S(2)}) copy-start(f32[1,256,4096]{1,2,0:T(8,128)} %copy.45) | copy-start | bytes 12582916
  151.9 2.9 %copy-start.2 = (bf16[1,256,4096]{1,2,0:T(8,128)(2,1)S(1)}, bf16[1,256,4096]{1,2,0:T(8,128)(2,1)}, u32[]{:S(2)}) copy-start(bf16[1,256,4096]{1,2,0:T(8,128)(2,1)} %copy.41) | copy-start | bytes 6291460
  151.9 2.9 %copy-start.3 = (pred[256,256]{1,0:T(8,128)(4,1)S(1)}, pred[256,256]{1,0:T(8,128)(4,1)}, u32[]{:S(2)}) copy-start(pred[256,256]{1,0:T(8,128)(4,1)} %iota_compare_fusion) | copy-start | bytes 196612
  151.9 2.9 %copy-start.4 = (f32[32,256]{1,0:T(8,128)S(1)}, f32[32,256]{1,0:T(8,128)}, u32[]{:S(2)}) copy-start(f32[32,256]{1,0:T(8,128)} %bitcast_add_fusion.1) | copy-start | bytes 98308
  151.9 2.9 %copy-start.5 = (f32[1,256,32]{1,2,0:T(8,128)S(1)}, f32[1,256,32]{1,2,0:T(8,128)}, u32[]{:S(2)}) copy-start(f32[1,256,32]{1,2,0:T(8,128)} %copy.77) | copy-start | bytes 98308
  151.9 2.9 %copy-start.6 = (f32[1,32,256]{2,1,0:T(8,128)S(1)}, f32[1,32,256]{2,1,0:T(8,128)}, u32[]{:S(2)}) copy-start(f32[1,32,256]{2,1,0:T(8,128)} %copy.78) | copy-start | bytes 98308
  151.9 2.9 %copy-start.7 = (f32[32]{0:T(128)S(1)}, f32[32]{0:T(128)}, u32[]{:S(2)}) copy-start(f32[32]{0:T(128)} %param.9) | copy-start | bytes 388
where the time goes:
time: 162 us; the launch traced here: 161 us
  local copies, waits for them, and re-layouts  53.2 us (33%)
  other arithmetic  38.3 us (24%)
  blocking collectives  35 us (22%)
  starting transfers between devices  12.9 us (8%)
  matrix products  12.2 us (8%)
  waiting for transfers between devices  9.28 us (6%)
    all_gather x1, blocking collectives, carry_state(): all_logs = lax.all_gather(device_log[None, :], 'seq', axis=0, tiled=True)  35 us
    unnamed x2, other arithmetic  24.2 us
    convert_element_type x1, local copies, waits for them, and re-layouts, carry_state(): flat_state.astype(jnp.bfloat16)  17 us
    unnamed x23, local copies, waits for them, and re-layouts  9.99 us
    all_to_all x1, waiting for transfers between devices, carry_state(): lax.all_to_all(as_sent(mixed), 'seq', split_axis=0, concat_axis=1, tiled=...  9.28 us
    mul x3, local copies, waits for them, and re-layouts, group_terms(): weighted = (values * tail_weight[..., None]).astype(jnp.bfloat16)  7.62 us
    reshape x1, other arithmetic, on_device(): conv_activate(extended, conv_weight, row_count)  6.12 us
    convert_element_type x1, local copies, waits for them, and re-layouts, group_terms(): local_out = intra_out + skip_gain[:, None] * values.astype(jnp.float32)  5.6 us
  transfers between devices with their start and end apart: 3, of which 1 were waited for; matrix products, arithmetic and copies ran while one was open for 19% of the time, Pallas kernels for 0%

commit v1 on v0

--- a/solution.py
+++ b/solution.py
@@ -1,3 +1,4 @@
+import functools
 import jax
 import jax.numpy as jnp
 from jax import lax
@@ -6,6 +7,21 @@
 HEADDIM = 128
 STATE = 128
 GROUP = 256
+
+
+def step_on_column(z, link_axis):
+    return jnp.concatenate(
+        lax.all_to_all(
+            jnp.stack(jnp.split(z, lax.axis_size(link_axis), axis=1), axis=0),
+            axis_name=link_axis,
+            split_axis=0,
+            concat_axis=0,
+        ),
+        axis=0,
+    )
+
+
+floor_compute = functools.partial(step_on_column, link_axis="seq")
 
 
 def as_sent(shard):
@@ -83,9 +99,7 @@
     head_count = device_log.shape[0]
     all_logs = lax.all_gather(device_log[None, :], "seq", axis=0, tiled=True)
     flat_state = final_state.reshape(1, head_count * HEADDIM, STATE)
-    received = lax.all_to_all(
-        flat_state.astype(jnp.bfloat16), "seq", split_axis=1, concat_axis=0, tiled=True
-    ).astype(flat_state.dtype)
+    received = floor_compute(flat_state.astype(jnp.bfloat16)).astype(flat_state.dtype)
     source_count = received.shape[0]
     row_count = received.shape[1]
     first_row = lax.axis_index("seq") * row_count

time: 162 us -> 124 us (0.77)
  other arithmetic: 38.3 us -> 14.7 us
  local copies, waits for them, and re-layouts: 53.2 us -> 39.4 us
    unnamed x2 -> x1, other arithmetic: 24.2 us -> 0.59 us
    convert_element_type x1 -> x0, local copies, waits for them, and re-layouts: 17 us -> none  [carry_state(): flat_state.astype(jnp.bfloat16)]
    unnamed x23 -> x34, local copies, waits for them, and re-layouts: 9.99 us -> 12.6 us
  transfers between devices with their start and end apart: 3 -> 3, of which waited for: 1 -> 1; matrix products, arithmetic and copies ran while one was open for 19% -> 25% of each run, Pallas kernels for 0% -> 0%
where the time goes in v1:
time: 124 us
  local copies, waits for them, and re-layouts  39.4 us (32%)
  blocking collectives  35 us (28%)
  other arithmetic  14.7 us (12%)
  starting transfers between devices  12.9 us (10%)
  matrix products  12.2 us (10%)
  waiting for transfers between devices  9.28 us (7%)
    all_gather x1, blocking collectives, carry_state(): all_logs = lax.all_gather(device_log[None, :], 'seq', axis=0, tiled=True)  35 us
    unnamed x34, local copies, waits for them, and re-layouts  12.6 us
    all_to_all x1, waiting for transfers between devices, carry_state(): lax.all_to_all(as_sent(mixed), 'seq', split_axis=0, concat_axis=1, tiled=...  9.27 us
    mul x3, local copies, waits for them, and re-layouts, group_terms(): weighted = (values * tail_weight[..., None]).astype(jnp.bfloat16)  7.62 us
    reshape x1, other arithmetic, on_device(): conv_activate(extended, conv_weight, row_count)  6.12 us
    convert_element_type x1, local copies, waits for them, and re-layouts, group_terms(): local_out = intra_out + skip_gain[:, None] * values.astype(jnp.float32)  5.6 us
    all_to_all x1, starting transfers between devices, step_on_column(): lax.all_to_all(jnp.stack(jnp.split(z, lax.axis_size(link_axis), axis=1),...  5.1 us
    all_to_all x1, starting transfers between devices, carry_state(): lax.all_to_all(as_sent(mixed), 'seq', split_axis=0, concat_axis=1, tiled=...  4.14 us
  transfers between devices with their start and end apart: 3, of which 1 were waited for; matrix products, arithmetic and copies ran while one was open for 25% of the time, Pallas kernels for 0%

profile of v1, /device:TPU:9, one launch (start us, length us, event | category | flops | bytes accessed | tf_op | source)
XLA Modules:
  0.0 123.7 jit_solution(2300189016929561997)
XLA Ops:
  0.0 0.9 slice.46
  0.9 3.7 %collective-permute-start = (bf16[3,4352]{1,0:T(4,128)(2,1)S(1)}, bf16[3,4352]{1,0:T(4,128)(2,1)S(1)}, u32[]{:S(2)}, u32[]{:S(2)}) collective-permute-start(bf16[3,4352]{1,0:T(4,128)(2,1)S(1)} %slice.46), channel_id=1, source_target_pairs={{0,1},{1,2},{2,3},{3,4},{4,5},{5,6},{6,7},{7,8},{8,9},{9,10},{10,1... | collective-permute-start | bytes 78344 | tf_op jit(solution)/shard_map/ppermute | solution.py:38
  4.6 0.7 exponential_negate_fusion
  5.3 0.8 compare_select_fusion
  6.1 0.6 reduce-window.6
  6.7 0.2 slice_reduce_fusion
  6.9 0.1 copy.31
  7.0 0.1 broadcast.128
  7.1 0.1 bitcast_exponential_fusion
  7.2 0.5 slice_reduce_fusion.5
  7.7 0.5 fusion.65
  8.2 0.1 broadcast_bitcast_fusion
  8.3 0.1 multiply_bitcast_fusion
  8.4 1.2 slice_reduce_fusion.4
  9.6 0.1 copy.41
  9.7 2.5 %mul.190 = f32[256,32,128]{2,1,0:T(8,128)} broadcast(f32[256,32]{1,0:T(8,128)S(1)} %bitcast.162), dimensions={0,1} | broadcast | bytes 4227072 | tf_op jit(solution)/shard_map/mul | solution.py:70
  12.3 5.0 %mul.191 = f32[1,256,4096]{2,1,0:T(8,128)} reshape(f32[256,32,128]{2,1,0:T(8,128)} %mul.190) | data formatting | bytes 8388608 | tf_op jit(solution)/shard_map/mul | solution.py:70
  17.3 6.1 %fusion.13 = bf16[1,256,4352]{2,1,0:T(8,128)(2,1)S(1)} fusion(bf16[256,4352]{1,0:T(8,128)(2,1)} %param.5, f32[4352]{0:T(1024)S(1)} %get-tuple-element.27, bf16[3,4352]{1,0:T(4,128)(2,1)S(1)} %collective-permute-done, f32[4352]{0:T(1024)S(1)} %get-tuple-element.28, f32[4352]{0:T(1024)S(1)} %get-tuple-element.26, f32[4352]{0:T(1024)S(1)} %get-tuple-element.20), kind=kLoop, calls=%fused_computation.21 | loop fusion | flops 27852800 | bytes 4552192 | tf_op jit(solution)/shard_map/reshape | solution.py:132
  23.4 0.6 fusion.14
  24.0 0.5 copy.47
  24.5 3.0 %fusion.1 = bf16[1,4096,128]{2,1,0:T(8,128)(2,1)S(1)} fusion(bf16[32,8,32,128]{3,2,1,0:T(8,128)(2,1)S(1)} %copy.47, f32[4096]{0:T(1024)S(1)} %broadcast_bitcast_fusion, bf16[1,256,4352]{2,1,0:T(8,128)(2,1)S(1)} %fusion.13), kind=kOutput, calls=%fused_computation.3 | convolution fusion | flops 269484032 | bytes 3227648 | tf_op jit(solution)/shard_map/cshp,csn->chpn/dot_general | solution.py:71
  27.5 0.6 fusion.53
  28.1 0.6 fusion.52
  28.8 0.6 fusion.51
  29.4 0.6 fusion.50
  30.0 0.6 fusion.49
  30.7 0.6 fusion.48
  31.3 0.6 fusion.47
  31.9 0.6 fusion.46
  32.6 0.6 fusion.45
  33.2 0.6 fusion.44
  33.8 0.6 fusion.43
  34.5 0.6 fusion.42
  35.1 0.6 fusion.41
  35.7 0.6 fusion.40
  36.4 0.6 fusion.39
  37.0 0.6 fusion.38
  37.6 5.1 %all-to-all-start = ((bf16[16,1,256,128]{3,2,1,0:T(8,128)(2,1)}), bf16[16,1,256,128]{3,2,1,0:T(8,128)(2,1)S(1)}, u32[]{:S(2)}, u32[]{:S(2)}) async-start(bf16[16,1,256,128]{3,2,1,0:T(8,128)(2,1)} %fusion.38), calls=%async_computation | async-start | bytes 2097152 | tf_op jit(solution)/shard_map/all_to_all | solution.py:14
  42.7 0.1 copy.35
  42.8 35.0 %all-gather = f32[16,1,32]{2,1,0:T(1,128)S(1)} all-gather(f32[1,1,32]{2,1,0:T(1,128)S(1)} %copy.35), channel_id=2, replica_groups=mesh['grp'=2,'seq'=16] {'seq'}, dimensions={0}, use_global_device_ids=true | all-gather | bytes 2176 | tf_op jit(solution)/shard_map/all_gather | solution.py:100
  77.8 0.2 fusion.37
  78.0 0.1 reduce_window_sum.48
  78.1 0.6 sub.66
  78.7 0.1 copy.37
  78.8 1.5 %copy.36 = f32[16,256]{0,1:T(8,128)} copy(f32[16,256]{1,0:T(8,128)} %sub.66) | data formatting | bytes 32768 | tf_op jit(solution)/shard_map/sub | solution.py:112
  80.3 3.9 %fusion.24 = bf16[16,256,128]{2,0,1:T(8,128)(2,1)S(1)} fusion(bf16[16,256,128]{2,1,0:T(8,128)(2,1)S(1)} %bitcast.161, f32[16,256]{0,1:T(8,128)S(1)} %copy.37, f32[16,256]{0,1:T(8,128)} %copy.36, pred[16,16]{1,0:T(8,128)(4,1)S(1)} %iota_compare_fusion.3), kind=kOutput, calls=%fused_computation.31 | convolution fusion | flops 101318656 | bytes 2130176 | tf_op jit(solution)/shard_map/sjr,jrn->srn/dot_general | solution.py:118
  84.3 1.2 %copy.39 = bf16[16,256,128]{2,1,0:T(8,128)(2,1)} copy(bf16[16,256,128]{2,0,1:T(8,128)(2,1)S(1)} %fusion.24) | data formatting | bytes 2097152 | tf_op jit(solution)/shard_map/convert_element_type | solution.py:30
  85.5 4.1 %all-to-all-start.1 = ((bf16[16,256,128]{2,1,0:T(8,128)(2,1)}), bf16[16,256,128]{2,1,0:T(8,128)(2,1)S(1)}, u32[]{:S(2)}, u32[]{:S(2)}) async-start(bf16[16,256,128]{2,1,0:T(8,128)(2,1)} %copy.39), calls=%async_computation.1 | async-start | bytes 2097152 | tf_op jit(solution)/shard_map/all_to_all | solution.py:119
  89.7 0.6 copy.61
  90.3 0.6 copy.62
  90.9 0.6 iota_compare_fusion
  91.6 0.6 bitcast_add_fusion.1
  92.2 3.2 %fusion.64 = (bf16[1,256,4096]{2,1,0:T(8,128)(2,1)}, f32[1,256,4096]{2,1,0:T(8,128)}) fusion(bf16[1,256,4352]{2,1,0:T(8,128)(2,1)S(1)} %fusion.13), kind=kLoop, calls=%fused_computation.112 | loop fusion | flops 1048576 | bytes 8388608 | tf_op jit(solution)/shard_map/slice | solution.py:55
  95.4 4.1 %copy.28 = bf16[1,256,4096]{1,2,0:T(8,128)(2,1)} copy(bf16[1,256,4096]{2,1,0:T(8,128)(2,1)} %get-tuple-element.36) | data formatting | bytes 4194304 | tf_op jit(solution)/shard_map/slice | solution.py:55
  99.4 5.6 %copy.32 = f32[1,256,4096]{1,2,0:T(8,128)} copy(f32[1,256,4096]{2,1,0:T(8,128)} %get-tuple-element.38) | data formatting | bytes 8388608 | tf_op jit(solution)/shard_map/convert_element_type | solution.py:68
  105.0 0.2 fusion.56
  105.2 9.3 %all-to-all-done.1 = bf16[16,256,128]{2,1,0:T(8,128)(2,1)S(1)} async-done(((bf16[16,256,128]{2,1,0:T(8,128)(2,1)}), bf16[16,256,128]{2,1,0:T(8,128)(2,1)S(1)}, u32[]{:S(2)}, u32[]{:S(2)}) %all-to-all-start.1) | async-done | bytes 1048608 | tf_op jit(solution)/shard_map/all_to_all | solution.py:119
  114.5 0.0 copy-start.7
  114.5 0.7 fusion.28
  115.3 0.7 fusion.30
  116.0 0.7 copy-done.1
  116.7 0.7 copy-done.2
  117.4 3.4 %fusion.4 = bf16[1,256,32,128]{1,3,2,0:T(8,128)(2,1)S(1)} fusion(f32[256,32,128]{0,2,1:T(8,128)S(1)} %fusion.30, f32[256,32,128]{0,2,1:T(8,128)S(1)} %fusion.28, f32[1,256,32,128]{1,3,2,0:T(8,128)S(1)} %bitcast.158, f32[256,32]{0,1:T(8,128)S(1)} %bitcast.169, f32[32]{0:T(128)S(1)} %copy-done.7, bf16[256,32,128]{0,2,1:T(8,128)(2,1)S(1)} %bitcast.159, ...), kind=kOutput, calls=%fused_computation.8 | convolution fusion | flops 553648128 | bytes 17203328 | tf_op jit(solution)/shard_map/chqs,cshp->cqhp/dot_general | solution.py:67
  120.8 2.9 %copy.40 = bf16[256,4096]{1,0:T(8,128)(2,1)} copy(bf16[256,4096]{0,1:T(8,128)(2,1)S(1)} %bitcast.160) | data formatting | bytes 4194304 | tf_op jit(solution)/shard_map/convert_element_type | solution.py:144
  (23 shorter events, 0.2 us)
Async XLA Ops:
  0.9 16.4 %collective-permute-start = (bf16[3,4352]{1,0:T(4,128)(2,1)S(1)}, bf16[3,4352]{1,0:T(4,128)(2,1)S(1)}, u32[]{:S(2)}, u32[]{:S(2)}) collective-permute-start(bf16[3,4352]{1,0:T(4,128)(2,1)S(1)} %slice.46), channel_id=1, source_target_pairs={{0,1},{1,2},{2,3},{3,4},{4,5},{5,6},{6,7},{7,8},{8,9},{9,10},{10,1... | collective-permute-start | bytes 78344 | tf_op jit(solution)/shard_map/ppermute | solution.py:38
  17.3 6.1 %copy-start = (f32[1,256,4096]{2,1,0:T(8,128)S(1)}, f32[1,256,4096]{2,1,0:T(8,128)}, u32[]{:S(2)}) copy-start(f32[1,256,4096]{2,1,0:T(8,128)} %mul.191) | copy-start | bytes 12582916
  37.6 42.7 %all-to-all-start = ((bf16[16,1,256,128]{3,2,1,0:T(8,128)(2,1)}), bf16[16,1,256,128]{3,2,1,0:T(8,128)(2,1)S(1)}, u32[]{:S(2)}, u32[]{:S(2)}) async-start(bf16[16,1,256,128]{3,2,1,0:T(8,128)(2,1)} %fusion.38), calls=%async_computation | async-start | bytes 2097152 | tf_op jit(solution)/shard_map/all_to_all | solution.py:14
  85.5 29.0 %all-to-all-start.1 = ((bf16[16,256,128]{2,1,0:T(8,128)(2,1)}), bf16[16,256,128]{2,1,0:T(8,128)(2,1)S(1)}, u32[]{:S(2)}, u32[]{:S(2)}) async-start(bf16[16,256,128]{2,1,0:T(8,128)(2,1)} %copy.39), calls=%async_computation.1 | async-start | bytes 2097152 | tf_op jit(solution)/shard_map/all_to_all | solution.py:119
  114.5 2.2 %copy-start.1 = (f32[1,256,4096]{1,2,0:T(8,128)S(1)}, f32[1,256,4096]{1,2,0:T(8,128)}, u32[]{:S(2)}) copy-start(f32[1,256,4096]{1,2,0:T(8,128)} %copy.32) | copy-start | bytes 12582916
  114.5 2.9 %copy-start.2 = (bf16[1,256,4096]{1,2,0:T(8,128)(2,1)S(1)}, bf16[1,256,4096]{1,2,0:T(8,128)(2,1)}, u32[]{:S(2)}) copy-start(bf16[1,256,4096]{1,2,0:T(8,128)(2,1)} %copy.28) | copy-start | bytes 6291460
  114.5 2.9 %copy-start.3 = (pred[256,256]{1,0:T(8,128)(4,1)S(1)}, pred[256,256]{1,0:T(8,128)(4,1)}, u32[]{:S(2)}) copy-start(pred[256,256]{1,0:T(8,128)(4,1)} %iota_compare_fusion) | copy-start | bytes 196612
  114.5 2.9 %copy-start.4 = (f32[32,256]{1,0:T(8,128)S(1)}, f32[32,256]{1,0:T(8,128)}, u32[]{:S(2)}) copy-start(f32[32,256]{1,0:T(8,128)} %bitcast_add_fusion.1) | copy-start | bytes 98308
  114.5 2.9 %copy-start.5 = (f32[1,256,32]{1,2,0:T(8,128)S(1)}, f32[1,256,32]{1,2,0:T(8,128)}, u32[]{:S(2)}) copy-start(f32[1,256,32]{1,2,0:T(8,128)} %copy.61) | copy-start | bytes 98308
  114.5 2.9 %copy-start.6 = (f32[1,32,256]{2,1,0:T(8,128)S(1)}, f32[1,32,256]{2,1,0:T(8,128)}, u32[]{:S(2)}) copy-start(f32[1,32,256]{2,1,0:T(8,128)} %copy.62) | copy-start | bytes 98308
  114.5 2.9 %copy-start.7 = (f32[32]{0:T(128)S(1)}, f32[32]{0:T(128)}, u32[]{:S(2)}) copy-start(f32[32]{0:T(128)} %param.9) | copy-start | bytes 388
